TPU v7x, 32 devices: a whole 2x2x4 slice. The times are simulated.
32 devices in a mesh: dp: 4 (over y, x), ctx: 8 (over z, core).
Axes of the slice: x: 2, y: 2, z: 4, core: 2. Of those that a mesh axis runs over, the one named last changes fastest.
Arguments:
- inputs: bfloat16 [4, 1024, 4096], P('dp', 'ctx'), may hold values from -8 to 8
- queries: bfloat16 [4, 1024, 8192], P('dp', 'ctx'), may hold values from -256 to 256
- grad_output: bfloat16 [4, 1024, 8192], P('dp', 'ctx'), may hold values from -6 to 6
- kv_weight: bfloat16 [4096, 1024], P(('dp', 'ctx')), may hold values from -1 to 1
Outputs:
- attn_out: bfloat16 [4, 1024, 8192], P('dp', 'ctx')
- grad_query: bfloat16 [4, 1024, 8192], P('dp', 'ctx')
- grad_inputs: bfloat16 [4, 1024, 4096], P('dp', 'ctx')
- grad_weight: float32 [4096, 1024], P(('dp', 'ctx'))
All inputs are finite; a program needn't handle non-finite values.
Results may differ from a plain program's by a relative error of at most 0.035.
Values may be sent and summed in bfloat16 or wider, within the bound.
No kernel may reach another device: no remote copies, remote signals or barrier semaphores. Data moves between devices by JAX's collectives and lax.ppermute only.
A program may use at most 128 MiB of HBM per device.

v0:
```python
import jax
import jax.numpy as jnp
from jax import lax
from jax.sharding import PartitionSpec as P

DH = 128
ROPE_BASE = 500000.0


def shifted(block, axis, distance):
    devices = range(lax.axis_size(axis))
    route = [(i - distance, i) for i in devices if i - distance in devices]
    return lax.ppermute(block, axis, route)


def shifted_2(value, axis, steps):
    count = lax.axis_size(axis)
    pairs = [(source, (source + steps) % count) for source in range(count)]
    return lax.ppermute(value, axis, pairs)


def rope_tables(positions, head_dim):
    half_dim = head_dim // 2
    frequency = ROPE_BASE ** (-2.0 * jnp.arange(half_dim, dtype=jnp.float32) / head_dim)
    angles = positions.astype(jnp.float32)[:, None] * frequency[None, :]
    return (jnp.cos(angles)[:, None, :], jnp.sin(angles)[:, None, :])


def rotary(values, positions):
    half_dim = values.shape[-1] // 2
    cosine, sine_table = rope_tables(positions, values.shape[-1])
    first_half = values[..., :half_dim]
    second = values[..., half_dim:]
    return jnp.concatenate(
        [first_half * cosine - second * sine_table, second * cosine + first_half * sine_table],
        axis=-1,
    )


def rotary_back(gradient, positions):
    half_dim = gradient.shape[-1] // 2
    cosine, sine_table = rope_tables(positions, gradient.shape[-1])
    first_half = gradient[..., :half_dim]
    second = gradient[..., half_dim:]
    return jnp.concatenate(
        [first_half * cosine + second * sine_table, second * cosine - first_half * sine_table],
        axis=-1,
    )


def on_device(inputs, queries, grad_output, kv_weight):
    token_count = inputs.shape[1]
    model_width = inputs.shape[2]
    kv_width = kv_weight.shape[1]
    kv_half = kv_width // 2
    head_dim = DH
    kv_heads = kv_half // head_dim
    q_heads = queries.shape[2] // head_dim
    group_size = q_heads // kv_heads
    row_count = group_size * token_count
    ctx_size = lax.axis_size("ctx")
    data_size = lax.axis_size("dp")
    ctx_index = lax.axis_index("ctx")
    score_scale = head_dim ** (-0.5)
    shard_rows = model_width // (data_size * ctx_size)
    tokens = inputs[0]
    weight_all = lax.all_gather(kv_weight, ("dp", "ctx"), axis=0, tiled=True)
    projected = jnp.dot(tokens, weight_all, preferred_element_type=jnp.float32)
    positions = ctx_index * token_count + jnp.arange(token_count, dtype=jnp.int32)
    key_rows = rotary(
        projected[:, :kv_half].reshape(token_count, kv_heads, head_dim), positions
    ).astype(jnp.bfloat16)
    value_rows = projected[:, kv_half:].astype(jnp.bfloat16)
    own_block = jnp.concatenate([key_rows.reshape(token_count, kv_half), value_rows], axis=1)

    def head_rows(matrix):
        return (
            matrix.reshape(token_count, kv_heads, group_size, head_dim)
            .transpose(1, 2, 0, 3)
            .reshape(kv_heads, row_count, head_dim)
        )

    def token_rows(rows_by_head):
        return (
            rows_by_head.reshape(kv_heads, group_size, token_count, head_dim)
            .transpose(2, 0, 1, 3)
            .reshape(token_count, q_heads * head_dim)
        )

    query_rows = head_rows(queries[0])
    grad_rows = head_rows(grad_output[0])
    query_pos = jnp.arange(row_count, dtype=jnp.int32) % token_count
    key_pos = jnp.arange(token_count, dtype=jnp.int32)

    def split_block(kv_block):
        key_part = kv_block[:, :kv_half].reshape(token_count, kv_heads, head_dim)
        value_part = kv_block[:, kv_half:].reshape(token_count, kv_heads, head_dim)
        return (key_part, value_part)

    def block_scores(key_part, block_id):
        scores = (
            jnp.einsum("hrd,khd->hrk", query_rows, key_part, preferred_element_type=jnp.float32)
            * score_scale
        )
        allowed = (block_id < ctx_index) | (query_pos[:, None] >= key_pos[None, :])
        return (scores, allowed)

    def forward_update(state_now, kv_block, block_id):
        row_top, row_total, row_accum = state_now
        key_part, value_part = split_block(kv_block)
        scores, allowed = block_scores(key_part, block_id)
        scores = jnp.where(allowed[None], scores, -jnp.inf)
        new_top = jnp.maximum(row_top, jnp.max(scores, axis=-1, keepdims=True))
        weights = jnp.exp(scores - new_top)
        factor = jnp.exp(row_top - new_top)
        row_total = row_total * factor + jnp.sum(weights, axis=-1, keepdims=True)
        row_accum = row_accum * factor + jnp.einsum(
            "hrk,khd->hrd",
            weights.astype(jnp.bfloat16),
            value_part,
            preferred_element_type=jnp.float32,
        )
        return (new_top, row_total, row_accum)

    start_state = (
        jnp.full((kv_heads, row_count, 1), -jnp.inf, jnp.float32),
        jnp.zeros((kv_heads, row_count, 1), jnp.float32),
        jnp.zeros((kv_heads, row_count, head_dim), jnp.float32),
    )
    state_now = forward_update(start_state, own_block, ctx_index)
    kv_store = jnp.zeros((ctx_size, token_count, kv_width), jnp.bfloat16)
    kv_store = lax.dynamic_update_slice_in_dim(kv_store, own_block[None], ctx_index, 0)

    def forward_step(offset, loop_state):
        kv_block, stored_now, state_here = loop_state
        kv_block = shifted(kv_block, "ctx", 1)
        source = ctx_index - offset

        def take_block(operands):
            stored, current = operands
            stored = lax.dynamic_update_slice_in_dim(stored, kv_block[None], source, 0)
            return (stored, forward_update(current, kv_block, source))

        def keep_state(operands):
            return operands

        stored_now, state_here = lax.cond(
            offset <= ctx_index, take_block, keep_state, (stored_now, state_here)
        )
        return (kv_block, stored_now, state_here)

    last_block, kv_store, state_now = lax.fori_loop(
        1, ctx_size, forward_step, (own_block, kv_store, state_now)
    )
    row_top, row_total, row_accum = state_now
    attn_rows = (row_accum / row_total).astype(jnp.bfloat16)
    log_total = row_top + jnp.log(row_total)
    row_delta = jnp.sum(
        grad_rows.astype(jnp.float32) * attn_rows.astype(jnp.float32), axis=-1, keepdims=True
    )
    attn_out = token_rows(attn_rows)[None]

    def backward_terms(kv_block, block_id):
        key_part, value_part = split_block(kv_block)
        scores, allowed = block_scores(key_part, block_id)
        probs_now = jnp.where(allowed[None], jnp.exp(scores - log_total), 0.0)
        dprobs = jnp.einsum(
            "hrd,khd->hrk", grad_rows, value_part, preferred_element_type=jnp.float32
        )
        dscores = (probs_now * (dprobs - row_delta)).astype(jnp.bfloat16)
        grad_keys = (
            jnp.einsum("hrk,hrd->khd", dscores, query_rows, preferred_element_type=jnp.float32)
            * score_scale
        )
        grad_values = jnp.einsum(
            "hrk,hrd->khd",
            probs_now.astype(jnp.bfloat16),
            grad_rows,
            preferred_element_type=jnp.float32,
        )
        query_part = jnp.einsum(
            "hrk,khd->hrd", dscores, key_part, preferred_element_type=jnp.float32
        )
        block_grads = jnp.concatenate(
            [grad_keys.reshape(token_count, kv_half), grad_values.reshape(token_count, kv_half)],
            axis=1,
        )
        return (block_grads, query_part)

    def add_block(operands, block_id):
        grad_block, grad_query_sum = operands
        kv_block = lax.dynamic_slice_in_dim(kv_store, block_id, 1, 0)[0]
        block_grads, query_part = backward_terms(kv_block, block_id)
        return (grad_block + block_grads, grad_query_sum + query_part)

    def skip_block(operand_pair):
        return operand_pair

    zero_grads = jnp.zeros((token_count, kv_width), jnp.float32)
    zero_query = jnp.zeros((kv_heads, row_count, head_dim), jnp.float32)

    def backward_step(offset, operands):
        source = ctx_index - offset

        def include(operand_pair):
            return add_block(operand_pair, source)

        grad_block, grad_query_sum = lax.cond(offset <= ctx_index, include, skip_block, operands)
        grad_block = shifted_2(grad_block.astype(jnp.bfloat16), "ctx", 1).astype(grad_block.dtype)
        return (grad_block, grad_query_sum)

    grad_block, grad_query_sum = lax.fori_loop(0, ctx_size, backward_step, (zero_grads, zero_query))
    grad_query = token_rows(grad_query_sum * score_scale).astype(jnp.bfloat16)[None]
    grad_key_rows = rotary_back(
        grad_block[:, :kv_half].reshape(token_count, kv_heads, head_dim), positions
    ).reshape(token_count, kv_half)
    grad_projected = jnp.concatenate([grad_key_rows, grad_block[:, kv_half:]], axis=1).astype(
        jnp.bfloat16
    )
    grad_inputs = lax.dot_general(
        grad_projected, weight_all, (((1,), (1,)), ((), ())), preferred_element_type=jnp.float32
    ).astype(jnp.bfloat16)[None]
    reordered = (
        tokens.reshape(token_count, data_size, ctx_size, shard_rows)
        .transpose(0, 2, 1, 3)
        .reshape(token_count, model_width)
    )
    partial_sum = lax.psum_scatter(
        lax.dot_general(
            reordered, grad_projected, (((0,), (0,)), ((), ())), preferred_element_type=jnp.float32
        ).astype(jnp.bfloat16),
        "ctx",
        scatter_dimension=0,
        tiled=True,
    )
    grad_weight = lax.psum_scatter(partial_sum, "dp", scatter_dimension=0, tiled=True).astype(
        jnp.float32
    )
    return (attn_out, grad_query, grad_inputs, grad_weight)


def solution(mesh):
    in_specs = (
        P("dp", "ctx", None),
        P("dp", "ctx", None),
        P("dp", "ctx", None),
        P(("dp", "ctx"), None),
    )
    out_specs = (
        P("dp", "ctx", None),
        P("dp", "ctx", None),
        P("dp", "ctx", None),
        P(("dp", "ctx"), None),
    )
    return jax.shard_map(
        on_device, mesh=mesh, in_specs=in_specs, out_specs=out_specs, check_vma=False
    )
```

profile of v0, /device:TPU:0, one launch (start us, length us, event | category | flops | bytes accessed | tf_op | source)
XLA Modules:
  0.0 496.9 jit_solution(8035987753920673615)
XLA Ops:
  8.0 3.5 copy.141
  11.5 4.3 copy.110
  15.8 2.3 reshape.240
  18.1 2.2 copy.139
  20.2 3.8 copy.102
  24.1 2.8 reshape.237
  26.9 2.5 copy.107
  29.4 2.3 copy.115
  31.6 2.3 copy.116
  35.2 55.6 %all-gather.2.cloned.1.call-done = bf16[4096,1024]{1,0:T(8,128)(2,1)} async-done(((bf16[128,1024]{1,0:T(8,128)(2,1)}), bf16[4096,1024]{1,0:T(8,128)(2,1)}) %all-gather.2.cloned.1.call-update) | async-done | bytes 8388624 | tf_op jit(solution)/shard_map/all_gather | solution.py:67
  90.8 5.0 fusion.27
  97.1 1.0 reshape.236
  98.6 1.8 fusion.36
  100.4 1.8 copy.106
  102.1 1.8 copy.101
  103.9 2.1 fusion.41
  106.7 3.3 convolution_add_fusion.1
  110.4 1.3 copy-done.5
  111.7 71.5 %while.38 = (s32[]{:T(128)}, bf16[128,1024]{0,1:T(8,128)(2,1)S(1)}, bf16[8,128,1024]{1,2,0:T(8,128)(2,1)}, f32[4,2048,1]{1,0,2:T(4,128)S(1)}, f32[4,2048,1]{1,0,...) while((s32[]{:T(128)}, bf16[128,1024]{0,1:T(8,128)(2,1)S(1)}, ...), condition=%wide.region_7.8_spmd.clone, body=%wide.region_2.7_spmd.clone.sunk | while | flops 551063552 | bytes 61154760 | solution.py:152
  111.7 2.2 collective-permute-start
  113.9 1.1 collective-permute-done
  115.0 15.1 %collective-permute-start = (bf16[128,1024]{0,1:T(8,128)(2,1)S(1)}, bf16[128,1024]{0,1:T(8,128)(2,1)S(1)}, u32[]{:S(2)}, u32[]{:S(2)}) collective-permute-start(bf16[128,1024]{0,1:T(8,128)(2,1)S(1)} %get-tuple-element.850), channel_id=1, source_target_pairs={{0,1},{1,2},{2,3},{3,4},{4,5},{5,6},{6,7},{8,9},{9,10},{10,11},{11... | collective-permute-start | bytes 786440 | tf_op jit(solution)/shard_map/while/body/eval_jaxpr/ppermute | solution.py:13
  130.2 1.1 collective-permute-done
  131.3 6.6 %collective-permute-start = (bf16[128,1024]{0,1:T(8,128)(2,1)S(1)}, bf16[128,1024]{0,1:T(8,128)(2,1)S(1)}, u32[]{:S(2)}, u32[]{:S(2)}) collective-permute-start(bf16[128,1024]{0,1:T(8,128)(2,1)S(1)} %get-tuple-element.850), channel_id=1, source_target_pairs={{0,1},{1,2},{2,3},{3,4},{4,5},{5,6},{6,7},{8,9},{9,10},{10,11},{11... | collective-permute-start | bytes 786440 | tf_op jit(solution)/shard_map/while/body/eval_jaxpr/ppermute | solution.py:13
  137.9 1.1 collective-permute-done
  139.0 16.2 %collective-permute-start = (bf16[128,1024]{0,1:T(8,128)(2,1)S(1)}, bf16[128,1024]{0,1:T(8,128)(2,1)S(1)}, u32[]{:S(2)}, u32[]{:S(2)}) collective-permute-start(bf16[128,1024]{0,1:T(8,128)(2,1)S(1)} %get-tuple-element.850), channel_id=1, source_target_pairs={{0,1},{1,2},{2,3},{3,4},{4,5},{5,6},{6,7},{8,9},{9,10},{10,11},{11... | collective-permute-start | bytes 786440 | tf_op jit(solution)/shard_map/while/body/eval_jaxpr/ppermute | solution.py:13
  155.3 1.1 collective-permute-done
  156.4 6.6 %collective-permute-start = (bf16[128,1024]{0,1:T(8,128)(2,1)S(1)}, bf16[128,1024]{0,1:T(8,128)(2,1)S(1)}, u32[]{:S(2)}, u32[]{:S(2)}) collective-permute-start(bf16[128,1024]{0,1:T(8,128)(2,1)S(1)} %get-tuple-element.850), channel_id=1, source_target_pairs={{0,1},{1,2},{2,3},{3,4},{4,5},{5,6},{6,7},{8,9},{9,10},{10,11},{11... | collective-permute-start | bytes 786440 | tf_op jit(solution)/shard_map/while/body/eval_jaxpr/ppermute | solution.py:13
  163.0 1.1 collective-permute-done
  164.2 10.2 %collective-permute-start = (bf16[128,1024]{0,1:T(8,128)(2,1)S(1)}, bf16[128,1024]{0,1:T(8,128)(2,1)S(1)}, u32[]{:S(2)}, u32[]{:S(2)}) collective-permute-start(bf16[128,1024]{0,1:T(8,128)(2,1)S(1)} %get-tuple-element.850), channel_id=1, source_target_pairs={{0,1},{1,2},{2,3},{3,4},{4,5},{5,6},{6,7},{8,9},{9,10},{10,11},{11... | collective-permute-start | bytes 786440 | tf_op jit(solution)/shard_map/while/body/eval_jaxpr/ppermute | solution.py:13
  174.3 1.1 collective-permute-done
  175.5 6.6 %collective-permute-start = (bf16[128,1024]{0,1:T(8,128)(2,1)S(1)}, bf16[128,1024]{0,1:T(8,128)(2,1)S(1)}, u32[]{:S(2)}, u32[]{:S(2)}) collective-permute-start(bf16[128,1024]{0,1:T(8,128)(2,1)S(1)} %get-tuple-element.850), channel_id=1, source_target_pairs={{0,1},{1,2},{2,3},{3,4},{4,5},{5,6},{6,7},{8,9},{9,10},{10,11},{11... | collective-permute-start | bytes 786440 | tf_op jit(solution)/shard_map/while/body/eval_jaxpr/ppermute | solution.py:13
  182.1 1.1 collective-permute-done
  183.2 5.4 %copy.108 = f32[4,2048,128]{1,2,0:T(8,128)} copy(f32[4,2048,128]{2,1,0:T(8,128)} %get-tuple-element.456) | data formatting | bytes 8388608 | tf_op jit(solution)/shard_map/while | solution.py:152
  188.7 5.0 %multiply_reduce_fusion = (f32[4,2048]{1,0:T(4,128)S(1)}, bf16[4,2048,128]{1,2,0:T(8,128)(2,1)}) fusion(bf16[4,2048,128]{1,2,0:T(8,128)(2,1)} %reshape.240, f32[4,2048,128]{1,2,0:T(8,128)} %copy.108, f32[4,2048]{1,0:T(4,128)S(1)} %bitcast.152), kind=kLoop, calls=%fused_computation.44 | loop fusion | flops 6283264 | bytes 8454144 | tf_op jit(solution)/shard_map/reduce_sum | solution.py:158
  193.7 2.2 broadcast.182
  195.9 169.3 %while.39 = (s32[]{:T(128)}, f32[128,1024]{0,1:T(8,128)S(1)}, f32[4,2048,128]{2,1,0:T(8,128)}, s32[]{:T(128)}, bf16[8,128,1024]{1,2,0:T(8,128)(2,1)}, /*index=5*...) while((s32[]{:T(128)}, f32[128,1024]{0,1:T(8,128)S(1)}, ...), condition=%wide.region_12.13_spmd.clone, body=%wide.region_9.12_spmd.clone.sunk | while | flops 1351823360 | bytes 85468640 | solution.py:212
  196.0 10.5 %conditional.7 = ((f32[128,1024]{0,1:T(8,128)S(1)}, f32[4,2048,128]{2,1,0:T(8,128)})) conditional(s32[]{:T(128)} %convert_element_type.142, (f32[128,1024]{0,1:T(8,128)S(1)}, f32[4,2048,128]{2,1,0:T(8,128)}) %tuple.112, (s32[]{:T(128)}, s32[]{:T(128)}, s32[2048]{0:T(1024)S(1)}, s32[128]{0:T(128)S(1)}, bf16[8,128,1024]{1,2,0:T(8,128)(2,1)}, ...), branch_computations={%region_10.10_spmd, %region_11.11_spmd.clone} | conditional | flops 1351428096 | bytes 81781416 | solution.py:208
  196.0 1.0 dynamic-slice_bitcast_fusion
  197.3 1.4 bitcast_select_fusion
  201.0 1.3 copy-done.3
  202.4 2.2 convolution_add_fusion
  204.6 1.9 copy-done.4
  206.5 14.3 %collective-permute-start.1 = (bf16[128,1024]{0,1:T(8,128)(2,1)S(1)}, bf16[128,1024]{0,1:T(8,128)(2,1)S(1)}, u32[]{:S(2)}, u32[]{:S(2)}) collective-permute-start(bf16[128,1024]{0,1:T(8,128)(2,1)S(1)} %convert_element_type.143), channel_id=1, source_target_pairs={{0,1},{1,2},{2,3},{3,4},{4,5},{5,6},{6,7},{7,0},{8,9},{9,10},{10,1... | collective-permute-start | bytes 786440 | tf_op jit(solution)/shard_map/while/body/eval_jaxpr/ppermute | solution.py:19
  220.9 37.2 %collective-permute-done.1 = bf16[128,1024]{0,1:T(8,128)(2,1)S(1)} collective-permute-done((bf16[128,1024]{0,1:T(8,128)(2,1)S(1)}, bf16[128,1024]{0,1:T(8,128)(2,1)S(1)}, u32[]{:S(2)}, u32[]{:S(2)}) %collective-permute-start.1) | collective-permute-done | bytes 262176 | tf_op jit(solution)/shard_map/while/body/eval_jaxpr/ppermute | solution.py:19
  258.3 13.8 %collective-permute-done.1 = bf16[128,1024]{0,1:T(8,128)(2,1)S(1)} collective-permute-done((bf16[128,1024]{0,1:T(8,128)(2,1)S(1)}, bf16[128,1024]{0,1:T(8,128)(2,1)S(1)}, u32[]{:S(2)}, u32[]{:S(2)}) %collective-permute-start.1) | collective-permute-done | bytes 262176 | tf_op jit(solution)/shard_map/while/body/eval_jaxpr/ppermute | solution.py:19
  272.4 13.8 %collective-permute-done.1 = bf16[128,1024]{0,1:T(8,128)(2,1)S(1)} collective-permute-done((bf16[128,1024]{0,1:T(8,128)(2,1)S(1)}, bf16[128,1024]{0,1:T(8,128)(2,1)S(1)}, u32[]{:S(2)}, u32[]{:S(2)}) %collective-permute-start.1) | collective-permute-done | bytes 262176 | tf_op jit(solution)/shard_map/while/body/eval_jaxpr/ppermute | solution.py:19
  286.5 13.8 %collective-permute-done.1 = bf16[128,1024]{0,1:T(8,128)(2,1)S(1)} collective-permute-done((bf16[128,1024]{0,1:T(8,128)(2,1)S(1)}, bf16[128,1024]{0,1:T(8,128)(2,1)S(1)}, u32[]{:S(2)}, u32[]{:S(2)}) %collective-permute-start.1) | collective-permute-done | bytes 262176 | tf_op jit(solution)/shard_map/while/body/eval_jaxpr/ppermute | solution.py:19
  300.6 14.8 %collective-permute-done.1 = bf16[128,1024]{0,1:T(8,128)(2,1)S(1)} collective-permute-done((bf16[128,1024]{0,1:T(8,128)(2,1)S(1)}, bf16[128,1024]{0,1:T(8,128)(2,1)S(1)}, u32[]{:S(2)}, u32[]{:S(2)}) %collective-permute-start.1) | collective-permute-done | bytes 262176 | tf_op jit(solution)/shard_map/while/body/eval_jaxpr/ppermute | solution.py:19
  315.7 16.3 %collective-permute-done.1 = bf16[128,1024]{0,1:T(8,128)(2,1)S(1)} collective-permute-done((bf16[128,1024]{0,1:T(8,128)(2,1)S(1)}, bf16[128,1024]{0,1:T(8,128)(2,1)S(1)}, u32[]{:S(2)}, u32[]{:S(2)}) %collective-permute-start.1) | collective-permute-done | bytes 262176 | tf_op jit(solution)/shard_map/while/body/eval_jaxpr/ppermute | solution.py:19
  332.3 16.3 %collective-permute-done.1 = bf16[128,1024]{0,1:T(8,128)(2,1)S(1)} collective-permute-done((bf16[128,1024]{0,1:T(8,128)(2,1)S(1)}, bf16[128,1024]{0,1:T(8,128)(2,1)S(1)}, u32[]{:S(2)}, u32[]{:S(2)}) %collective-permute-start.1) | collective-permute-done | bytes 262176 | tf_op jit(solution)/shard_map/while/body/eval_jaxpr/ppermute | solution.py:19
  348.9 16.3 %collective-permute-done.1 = bf16[128,1024]{0,1:T(8,128)(2,1)S(1)} collective-permute-done((bf16[128,1024]{0,1:T(8,128)(2,1)S(1)}, bf16[128,1024]{0,1:T(8,128)(2,1)S(1)}, u32[]{:S(2)}, u32[]{:S(2)}) %collective-permute-start.1) | collective-permute-done | bytes 262176 | tf_op jit(solution)/shard_map/while/body/eval_jaxpr/ppermute | solution.py:19
  366.4 5.6 %convert_bitcast_fusion = bf16[4096,1024]{0,1:T(8,128)(2,1)} fusion(bf16[128,4096]{0,1:T(8,128)(2,1)S(1)} %bitcast.151, bf16[128,512]{0,1:T(8,128)(2,1)S(1)} %slice.61, bf16[128,512]{0,1:T(8,128)(2,1)S(1)} %bitcast.158), kind=kOutput, calls=%fused_computation.39 | convolution fusion | flops 1078460416 | bytes 9699328 | tf_op jit(solution)/shard_map/dot_general | solution.py:229
  372.1 86.9 %reduce-scatter.5.cloned.1.call-done = bf16[512,1024]{0,1:T(8,128)(2,1)} async-done(((bf16[4096,1024]{0,1:T(8,128)(2,1)}), bf16[512,1024]{0,1:T(8,128)(2,1)}) %reduce-scatter.5.cloned.1.call-update) | async-done | bytes 1048592 | tf_op jit(solution)/shard_map/reduce_scatter | solution.py:228
  458.9 2.3 copy.131
  461.3 2.2 copy.140
  463.5 3.8 copy.109
  467.2 4.2 broadcast_in_dim_reshape.3
  471.4 2.8 multiply_convert_fusion
  474.2 1.4 copy.152
  475.6 2.3 convert_element_type.107
  477.9 7.3 %fusion.22 = bf16[1,128,4096]{2,1,0:T(8,128)(2,1)} fusion(bf16[4096,1024]{1,0:T(8,128)(2,1)} %all-gather.2.cloned.1.call-done, bf16[128,512]{0,1:T(8,128)(2,1)S(1)} %slice.61, bf16[128,512]{0,1:T(8,128)(2,1)S(1)} %bitcast.159), kind=kOutput, calls=%fused_computation.41 | convolution fusion | flops 1074790400 | bytes 9699328 | tf_op jit(solution)/shard_map/dot_general | solution.py:220
  485.1 3.2 reduce-scatter.7.cloned.1.call-done
  488.3 1.1 copy.132
  (155 shorter events, 11.1 us)
Async XLA Ops:
  7.2 83.6 %all-gather.2.cloned.1.call-start = ((), (), s32[]{:S(2)}) async-start(), calls=%async_computation.2 | async-start | bytes 8650752 | tf_op jit(solution)/shard_map/all_gather | solution.py:67
  7.9 451.1 %reduce-scatter.5.cloned.1.call-start = ((), (), s32[]{:S(2)}) async-start(), calls=%async_computation.3 | async-start | bytes 9437184 | tf_op jit(solution)/shard_map/reduce_scatter | solution.py:228
  34.3 64.1 %copy-start.8 = (f32[128,64]{1,0:T(8,128)}, f32[128,64]{1,0:T(8,128)S(1)}, u32[]{:S(2)}) copy-start(f32[128,64]{1,0:T(8,128)S(1)} %get-tuple-element.707) | copy-start | bytes 98308
  34.3 64.1 %copy-start.10 = (f32[128,64]{1,0:T(8,128)}, f32[128,64]{1,0:T(8,128)S(1)}, u32[]{:S(2)}) copy-start(f32[128,64]{1,0:T(8,128)S(1)} %get-tuple-element.708) | copy-start | bytes 98308
  106.7 3.6 copy-start.7
  106.7 5.0 copy-start.12
  110.4 1.3 copy-start.5
  111.7 3.3 collective-permute-start
  115.0 16.2 %collective-permute-start = (bf16[128,1024]{0,1:T(8,128)(2,1)S(1)}, bf16[128,1024]{0,1:T(8,128)(2,1)S(1)}, u32[]{:S(2)}, u32[]{:S(2)}) collective-permute-start(bf16[128,1024]{0,1:T(8,128)(2,1)S(1)} %get-tuple-element.850), channel_id=1, source_target_pairs={{0,1},{1,2},{2,3},{3,4},{4,5},{5,6},{6,7},{8,9},{9,10},{10,11},{11... | collective-permute-start | bytes 786440 | tf_op jit(solution)/shard_map/while/body/eval_jaxpr/ppermute | solution.py:13
  131.3 7.7 %collective-permute-start = (bf16[128,1024]{0,1:T(8,128)(2,1)S(1)}, bf16[128,1024]{0,1:T(8,128)(2,1)S(1)}, u32[]{:S(2)}, u32[]{:S(2)}) collective-permute-start(bf16[128,1024]{0,1:T(8,128)(2,1)S(1)} %get-tuple-element.850), channel_id=1, source_target_pairs={{0,1},{1,2},{2,3},{3,4},{4,5},{5,6},{6,7},{8,9},{9,10},{10,11},{11... | collective-permute-start | bytes 786440 | tf_op jit(solution)/shard_map/while/body/eval_jaxpr/ppermute | solution.py:13
  139.0 17.3 %collective-permute-start = (bf16[128,1024]{0,1:T(8,128)(2,1)S(1)}, bf16[128,1024]{0,1:T(8,128)(2,1)S(1)}, u32[]{:S(2)}, u32[]{:S(2)}) collective-permute-start(bf16[128,1024]{0,1:T(8,128)(2,1)S(1)} %get-tuple-element.850), channel_id=1, source_target_pairs={{0,1},{1,2},{2,3},{3,4},{4,5},{5,6},{6,7},{8,9},{9,10},{10,11},{11... | collective-permute-start | bytes 786440 | tf_op jit(solution)/shard_map/while/body/eval_jaxpr/ppermute | solution.py:13
  156.4 7.7 %collective-permute-start = (bf16[128,1024]{0,1:T(8,128)(2,1)S(1)}, bf16[128,1024]{0,1:T(8,128)(2,1)S(1)}, u32[]{:S(2)}, u32[]{:S(2)}) collective-permute-start(bf16[128,1024]{0,1:T(8,128)(2,1)S(1)} %get-tuple-element.850), channel_id=1, source_target_pairs={{0,1},{1,2},{2,3},{3,4},{4,5},{5,6},{6,7},{8,9},{9,10},{10,11},{11... | collective-permute-start | bytes 786440 | tf_op jit(solution)/shard_map/while/body/eval_jaxpr/ppermute | solution.py:13
  164.2 11.3 %collective-permute-start = (bf16[128,1024]{0,1:T(8,128)(2,1)S(1)}, bf16[128,1024]{0,1:T(8,128)(2,1)S(1)}, u32[]{:S(2)}, u32[]{:S(2)}) collective-permute-start(bf16[128,1024]{0,1:T(8,128)(2,1)S(1)} %get-tuple-element.850), channel_id=1, source_target_pairs={{0,1},{1,2},{2,3},{3,4},{4,5},{5,6},{6,7},{8,9},{9,10},{10,11},{11... | collective-permute-start | bytes 786440 | tf_op jit(solution)/shard_map/while/body/eval_jaxpr/ppermute | solution.py:13
  175.5 7.7 %collective-permute-start = (bf16[128,1024]{0,1:T(8,128)(2,1)S(1)}, bf16[128,1024]{0,1:T(8,128)(2,1)S(1)}, u32[]{:S(2)}, u32[]{:S(2)}) collective-permute-start(bf16[128,1024]{0,1:T(8,128)(2,1)S(1)} %get-tuple-element.850), channel_id=1, source_target_pairs={{0,1},{1,2},{2,3},{3,4},{4,5},{5,6},{6,7},{8,9},{9,10},{10,11},{11... | collective-permute-start | bytes 786440 | tf_op jit(solution)/shard_map/while/body/eval_jaxpr/ppermute | solution.py:13
  195.9 169.7 %copy-start.9 = (f32[128,64]{1,0:T(8,128)S(1)}, f32[128,64]{1,0:T(8,128)}, u32[]{:S(2)}) copy-start(f32[128,64]{1,0:T(8,128)} %copy-done.8) | copy-start | bytes 98308
  195.9 169.7 %copy-start.11 = (f32[128,64]{1,0:T(8,128)S(1)}, f32[128,64]{1,0:T(8,128)}, u32[]{:S(2)}) copy-start(f32[128,64]{1,0:T(8,128)} %copy-done.10) | copy-start | bytes 98308
  197.0 1.7 copy-start
  200.2 2.2 copy-start.3
  204.6 1.9 copy-start.4
  206.5 51.5 %collective-permute-start.1 = (bf16[128,1024]{0,1:T(8,128)(2,1)S(1)}, bf16[128,1024]{0,1:T(8,128)(2,1)S(1)}, u32[]{:S(2)}, u32[]{:S(2)}) collective-permute-start(bf16[128,1024]{0,1:T(8,128)(2,1)S(1)} %convert_element_type.143), channel_id=1, source_target_pairs={{0,1},{1,2},{2,3},{3,4},{4,5},{5,6},{6,7},{7,0},{8,9},{9,10},{10,1... | collective-permute-start | bytes 786440 | tf_op jit(solution)/shard_map/while/body/eval_jaxpr/ppermute | solution.py:19
  258.3 13.9 %collective-permute-start.1 = (bf16[128,1024]{0,1:T(8,128)(2,1)S(1)}, bf16[128,1024]{0,1:T(8,128)(2,1)S(1)}, u32[]{:S(2)}, u32[]{:S(2)}) collective-permute-start(bf16[128,1024]{0,1:T(8,128)(2,1)S(1)} %convert_element_type.143), channel_id=1, source_target_pairs={{0,1},{1,2},{2,3},{3,4},{4,5},{5,6},{6,7},{7,0},{8,9},{9,10},{10,1... | collective-permute-start | bytes 786440 | tf_op jit(solution)/shard_map/while/body/eval_jaxpr/ppermute | solution.py:19
  272.4 13.9 %collective-permute-start.1 = (bf16[128,1024]{0,1:T(8,128)(2,1)S(1)}, bf16[128,1024]{0,1:T(8,128)(2,1)S(1)}, u32[]{:S(2)}, u32[]{:S(2)}) collective-permute-start(bf16[128,1024]{0,1:T(8,128)(2,1)S(1)} %convert_element_type.143), channel_id=1, source_target_pairs={{0,1},{1,2},{2,3},{3,4},{4,5},{5,6},{6,7},{7,0},{8,9},{9,10},{10,1... | collective-permute-start | bytes 786440 | tf_op jit(solution)/shard_map/while/body/eval_jaxpr/ppermute | solution.py:19
  286.5 13.9 %collective-permute-start.1 = (bf16[128,1024]{0,1:T(8,128)(2,1)S(1)}, bf16[128,1024]{0,1:T(8,128)(2,1)S(1)}, u32[]{:S(2)}, u32[]{:S(2)}) collective-permute-start(bf16[128,1024]{0,1:T(8,128)(2,1)S(1)} %convert_element_type.143), channel_id=1, source_target_pairs={{0,1},{1,2},{2,3},{3,4},{4,5},{5,6},{6,7},{7,0},{8,9},{9,10},{10,1... | collective-permute-start | bytes 786440 | tf_op jit(solution)/shard_map/while/body/eval_jaxpr/ppermute | solution.py:19
  300.5 14.9 %collective-permute-start.1 = (bf16[128,1024]{0,1:T(8,128)(2,1)S(1)}, bf16[128,1024]{0,1:T(8,128)(2,1)S(1)}, u32[]{:S(2)}, u32[]{:S(2)}) collective-permute-start(bf16[128,1024]{0,1:T(8,128)(2,1)S(1)} %convert_element_type.143), channel_id=1, source_target_pairs={{0,1},{1,2},{2,3},{3,4},{4,5},{5,6},{6,7},{7,0},{8,9},{9,10},{10,1... | collective-permute-start | bytes 786440 | tf_op jit(solution)/shard_map/while/body/eval_jaxpr/ppermute | solution.py:19
  315.7 16.4 %collective-permute-start.1 = (bf16[128,1024]{0,1:T(8,128)(2,1)S(1)}, bf16[128,1024]{0,1:T(8,128)(2,1)S(1)}, u32[]{:S(2)}, u32[]{:S(2)}) collective-permute-start(bf16[128,1024]{0,1:T(8,128)(2,1)S(1)} %convert_element_type.143), channel_id=1, source_target_pairs={{0,1},{1,2},{2,3},{3,4},{4,5},{5,6},{6,7},{7,0},{8,9},{9,10},{10,1... | collective-permute-start | bytes 786440 | tf_op jit(solution)/shard_map/while/body/eval_jaxpr/ppermute | solution.py:19
  332.2 16.4 %collective-permute-start.1 = (bf16[128,1024]{0,1:T(8,128)(2,1)S(1)}, bf16[128,1024]{0,1:T(8,128)(2,1)S(1)}, u32[]{:S(2)}, u32[]{:S(2)}) collective-permute-start(bf16[128,1024]{0,1:T(8,128)(2,1)S(1)} %convert_element_type.143), channel_id=1, source_target_pairs={{0,1},{1,2},{2,3},{3,4},{4,5},{5,6},{6,7},{7,0},{8,9},{9,10},{10,1... | collective-permute-start | bytes 786440 | tf_op jit(solution)/shard_map/while/body/eval_jaxpr/ppermute | solution.py:19
  348.8 16.4 %collective-permute-start.1 = (bf16[128,1024]{0,1:T(8,128)(2,1)S(1)}, bf16[128,1024]{0,1:T(8,128)(2,1)S(1)}, u32[]{:S(2)}, u32[]{:S(2)}) collective-permute-start(bf16[128,1024]{0,1:T(8,128)(2,1)S(1)} %convert_element_type.143), channel_id=1, source_target_pairs={{0,1},{1,2},{2,3},{3,4},{4,5},{5,6},{6,7},{7,0},{8,9},{9,10},{10,1... | collective-permute-start | bytes 786440 | tf_op jit(solution)/shard_map/while/body/eval_jaxpr/ppermute | solution.py:19
  365.2 1.2 copy-start.6
  372.0 116.3 %reduce-scatter.7.cloned.1.call-start = ((), (), s32[]{:S(2)}) async-start(), calls=%async_computation.4 | async-start | bytes 1310720
Sparse Core Ops, SparseCore 0:
  11.0 79.7 all-gather.1
  372.2 86.7 reduce-scatter.4
  461.8 26.4 reduce-scatter.6
where the time goes:
time: 498 us; the launch traced here: 497 us
  waiting for transfers between devices  297 us (60%)
  starting transfers between devices  78.1 us (16%)
  local copies, waits for them, and re-layouts  65 us (13%)
  matrix products  29 us (6%)
  between operations  14 us (3%)
  other arithmetic  13.1 us (3%)
    ppermute x8, waiting for transfers between devices, shifted_2(): return lax.ppermute(value, axis, pairs)  142 us
    reduce_scatter x1, waiting for transfers between devices, on_device(): lax.psum_scatter(lax.dot_general(reordered, grad_projected, (((0,), (0,))...  86.9 us
    ppermute x7, starting transfers between devices, shifted(): return lax.ppermute(block, axis, route)  63.3 us
    all_gather x1, waiting for transfers between devices, on_device(): weight_all = lax.all_gather(kv_weight, ('dp', 'ctx'), axis=0, tiled=True)  55.6 us
    unnamed x27, local copies, waits for them, and re-layouts  20.9 us
    ppermute x8, starting transfers between devices, shifted_2(): return lax.ppermute(value, axis, pairs)  14.7 us
  transfers between devices with their start and end apart: 18, of which 18 were waited for; matrix products, arithmetic and copies ran while one was open for 10% of the time, Pallas kernels for 0%

commit v1 on v0

--- a/solution.py
+++ b/solution.py
@@ -64,7 +64,16 @@
     score_scale = head_dim ** (-0.5)
     shard_rows = model_width // (data_size * ctx_size)
     tokens = inputs[0]
-    weight_all = lax.all_gather(kv_weight, ("dp", "ctx"), axis=0, tiled=True)
+    shaped, r1 = (jax.lax.axis_size(("dp", "ctx")), jax.lax.axis_index(("dp", "ctx")))
+    weight_all, f_next = (kv_weight, 1)
+    while f_next < shaped:
+        all_values = jax.lax.ppermute(
+            weight_all, ("dp", "ctx"), [(it, it ^ f_next) for it in range(shaped)]
+        )
+        step_out = jnp.concatenate([weight_all, all_values], axis=0)
+        val2 = jnp.concatenate([all_values, weight_all], axis=0)
+        weight_all = jnp.where(r1 & f_next == 0, step_out, val2)
+        f_next = 2 * f_next
     projected = jnp.dot(tokens, weight_all, preferred_element_type=jnp.float32)
     positions = ctx_index * token_count + jnp.arange(token_count, dtype=jnp.int32)
     key_rows = rotary(

time: 498 us -> 629 us (1.26)
  waiting for transfers between devices: 297 us -> 412 us
  other arithmetic: 13.1 us -> 22.1 us
  starting transfers between devices: 78.1 us -> 85.1 us
    ppermute x0 -> x5, waiting for transfers between devices: none -> 167 us  [on_device(): jax.lax.ppermute(weight_all, ('dp', 'ctx'), [(it, it ^ f_next) for it in...]
    all_gather x1 -> x0, waiting for transfers between devices: 55.6 us -> none  [on_device(): weight_all = lax.all_gather(kv_weight, ('dp', 'ctx'), axis=0, tiled=True)]
    select_n x0 -> x4, other arithmetic: none -> 9.2 us  [on_device(): weight_all = jnp.where(r1 & f_next == 0, step_out, val2)]
    ppermute x0 -> x5, starting transfers between devices: none -> 9.1 us  [on_device(): jax.lax.ppermute(weight_all, ('dp', 'ctx'), [(it, it ^ f_next) for it in...]
    unnamed x27 -> x18, local copies, waits for them, and re-layouts: 20.9 us -> 19 us
  transfers between devices with their start and end apart: 18 -> 22, of which waited for: 18 -> 22; matrix products, arithmetic and copies ran while one was open for 10% -> 8% of each run, Pallas kernels for 0% -> 0%
where the time goes in v1:
time: 629 us; the launch traced here: 628 us
  waiting for transfers between devices  412 us (66%)
  starting transfers between devices  85.1 us (14%)
  local copies, waits for them, and re-layouts  60.9 us (10%)
  matrix products  32.2 us (5%)
  other arithmetic  22.1 us (4%)
  between operations  14.3 us (2%)
    ppermute x5, waiting for transfers between devices, on_device(): jax.lax.ppermute(weight_all, ('dp', 'ctx'), [(it, it ^ f_next) for it in...  167 us
    ppermute x8, waiting for transfers between devices, shifted_2(): return lax.ppermute(value, axis, pairs)  148 us
    reduce_scatter x1, waiting for transfers between devices, on_device(): lax.psum_scatter(lax.dot_general(reordered, grad_projected, (((0,), (0,))...  87.8 us
    ppermute x7, starting transfers between devices, shifted(): return lax.ppermute(block, axis, route)  61.2 us
    unnamed x18, local copies, waits for them, and re-layouts  19 us
    ppermute x8, starting transfers between devices, shifted_2(): return lax.ppermute(value, axis, pairs)  14.7 us
  transfers between devices with their start and end apart: 22, of which 22 were waited for; matrix products, arithmetic and copies ran while one was open for 8% of the time, Pallas kernels for 0%

profile of v1, /device:TPU:0, one launch (start us, length us, event | category | flops | bytes accessed | tf_op | source)
XLA Modules:
  0.0 627.6 jit_solution(3290680269114695586)
XLA Ops:
  7.8 1.4 collective-permute-done.2
  9.1 1.3 maximum_select_fusion.8
  10.4 3.0 collective-permute-start.3
  13.4 12.2 %collective-permute-done.3 = bf16[256,1024]{1,0:T(8,128)(2,1)S(1)} collective-permute-done((bf16[256,1024]{1,0:T(8,128)(2,1)S(1)}, bf16[256,1024]{1,0:T(8,128)(2,1)S(1)}, u32[]{:S(2)}, u32[]{:S(2)}) %collective-permute-start.3) | collective-permute-done | bytes 524320 | tf_op jit(solution)/shard_map/ppermute | solution.py:70
  26.1 2.8 collective-permute-start.4
  28.9 45.3 %collective-permute-done.4 = bf16[512,1024]{1,0:T(8,128)(2,1)} collective-permute-done((bf16[512,1024]{1,0:T(8,128)(2,1)S(1)}, bf16[512,1024]{1,0:T(8,128)(2,1)}, u32[]{:S(2)}, u32[]{:S(2)}) %collective-permute-start.4) | collective-permute-done | bytes 1048608 | tf_op jit(solution)/shard_map/ppermute | solution.py:70
  74.3 2.5 maximum_select_fusion.2
  76.8 1.4 collective-permute-start.5
  78.3 45.4 %collective-permute-done.5 = bf16[1024,1024]{1,0:T(8,128)(2,1)} collective-permute-done((bf16[1024,1024]{1,0:T(8,128)(2,1)S(1)}, bf16[1024,1024]{1,0:T(8,128)(2,1)}, u32[]{:S(2)}, u32[]{:S(2)}) %collective-permute-start.5) | collective-permute-done | bytes 2097184 | tf_op jit(solution)/shard_map/ppermute | solution.py:70
  123.7 4.9 maximum_select_fusion.1
  128.6 1.3 collective-permute-start.6
  129.9 3.5 copy.136
  133.4 4.3 copy.106
  137.7 2.3 reshape.240
  140.0 2.2 copy.134
  142.2 3.8 copy.99
  146.0 2.8 reshape.237
  148.8 2.6 copy.103
  151.4 2.3 copy.111
  153.6 2.3 copy.112
  157.1 62.6 %collective-permute-done.6 = bf16[2048,1024]{1,0:T(8,128)(2,1)} collective-permute-done((bf16[2048,1024]{1,0:T(8,128)(2,1)}, bf16[2048,1024]{1,0:T(8,128)(2,1)}, u32[]{:S(2)}, u32[]{:S(2)}) %collective-permute-start.6) | collective-permute-done | bytes 4194336 | tf_op jit(solution)/shard_map/ppermute | solution.py:70
  219.6 7.6 %fusion.28 = f32[128,1024]{0,1:T(8,128)S(1)} fusion(bf16[2048,1024]{1,0:T(8,128)(2,1)} %collective-permute-done.6, bf16[2048,1024]{1,0:T(8,128)(2,1)} %maximum_select_fusion.1, pred[]{:T(512)S(6)} %eq.17, bf16[1,128,4096]{2,1,0:T(8,128)(2,1)} %param.12), kind=kOutput, calls=%fused_computation.56 | convolution fusion | flops 1111490560 | bytes 9961473 | tf_op jit(solution)/shard_map/dot_general | solution.py:77
  232.0 1.6 broadcast_in_dim.82
  234.3 3.2 convolution_add_fusion.1
  237.6 69.4 %while.38 = (s32[]{:T(128)}, bf16[128,1024]{0,1:T(8,128)(2,1)S(1)}, bf16[8,128,1024]{1,2,0:T(8,128)(2,1)}, f32[4,2048,1]{1,0,2:T(4,128)S(1)}, f32[4,2048,1]{1,0,...) while((s32[]{:T(128)}, bf16[128,1024]{0,1:T(8,128)(2,1)S(1)}, ...), condition=%wide.region_7.8_spmd.clone, body=%wide.region_2.7_spmd.clone.sunk | while | flops 551063552 | bytes 61154760 | solution.py:161
  237.6 1.3 collective-permute-start
  240.0 16.7 %collective-permute-start = (bf16[128,1024]{0,1:T(8,128)(2,1)S(1)}, bf16[128,1024]{0,1:T(8,128)(2,1)S(1)}, u32[]{:S(2)}, u32[]{:S(2)}) collective-permute-start(bf16[128,1024]{0,1:T(8,128)(2,1)S(1)} %get-tuple-element.848), channel_id=1, source_target_pairs={{0,1},{1,2},{2,3},{3,4},{4,5},{5,6},{6,7},{8,9},{9,10},{10,11},{11... | collective-permute-start | bytes 786440 | tf_op jit(solution)/shard_map/while/body/eval_jaxpr/ppermute | solution.py:13
  257.9 6.6 %collective-permute-start = (bf16[128,1024]{0,1:T(8,128)(2,1)S(1)}, bf16[128,1024]{0,1:T(8,128)(2,1)S(1)}, u32[]{:S(2)}, u32[]{:S(2)}) collective-permute-start(bf16[128,1024]{0,1:T(8,128)(2,1)S(1)} %get-tuple-element.848), channel_id=1, source_target_pairs={{0,1},{1,2},{2,3},{3,4},{4,5},{5,6},{6,7},{8,9},{9,10},{10,11},{11... | collective-permute-start | bytes 786440 | tf_op jit(solution)/shard_map/while/body/eval_jaxpr/ppermute | solution.py:13
  264.5 1.1 collective-permute-done
  265.6 16.2 %collective-permute-start = (bf16[128,1024]{0,1:T(8,128)(2,1)S(1)}, bf16[128,1024]{0,1:T(8,128)(2,1)S(1)}, u32[]{:S(2)}, u32[]{:S(2)}) collective-permute-start(bf16[128,1024]{0,1:T(8,128)(2,1)S(1)} %get-tuple-element.848), channel_id=1, source_target_pairs={{0,1},{1,2},{2,3},{3,4},{4,5},{5,6},{6,7},{8,9},{9,10},{10,11},{11... | collective-permute-start | bytes 786440 | tf_op jit(solution)/shard_map/while/body/eval_jaxpr/ppermute | solution.py:13
  281.9 1.1 collective-permute-done
  283.0 6.6 %collective-permute-start = (bf16[128,1024]{0,1:T(8,128)(2,1)S(1)}, bf16[128,1024]{0,1:T(8,128)(2,1)S(1)}, u32[]{:S(2)}, u32[]{:S(2)}) collective-permute-start(bf16[128,1024]{0,1:T(8,128)(2,1)S(1)} %get-tuple-element.848), channel_id=1, source_target_pairs={{0,1},{1,2},{2,3},{3,4},{4,5},{5,6},{6,7},{8,9},{9,10},{10,11},{11... | collective-permute-start | bytes 786440 | tf_op jit(solution)/shard_map/while/body/eval_jaxpr/ppermute | solution.py:13
  290.7 7.4 %collective-permute-start = (bf16[128,1024]{0,1:T(8,128)(2,1)S(1)}, bf16[128,1024]{0,1:T(8,128)(2,1)S(1)}, u32[]{:S(2)}, u32[]{:S(2)}) collective-permute-start(bf16[128,1024]{0,1:T(8,128)(2,1)S(1)} %get-tuple-element.848), channel_id=1, source_target_pairs={{0,1},{1,2},{2,3},{3,4},{4,5},{5,6},{6,7},{8,9},{9,10},{10,11},{11... | collective-permute-start | bytes 786440 | tf_op jit(solution)/shard_map/while/body/eval_jaxpr/ppermute | solution.py:13
  299.3 6.6 %collective-permute-start = (bf16[128,1024]{0,1:T(8,128)(2,1)S(1)}, bf16[128,1024]{0,1:T(8,128)(2,1)S(1)}, u32[]{:S(2)}, u32[]{:S(2)}) collective-permute-start(bf16[128,1024]{0,1:T(8,128)(2,1)S(1)} %get-tuple-element.848), channel_id=1, source_target_pairs={{0,1},{1,2},{2,3},{3,4},{4,5},{5,6},{6,7},{8,9},{9,10},{10,11},{11... | collective-permute-start | bytes 786440 | tf_op jit(solution)/shard_map/while/body/eval_jaxpr/ppermute | solution.py:13
  307.0 5.5 copy.104
  312.5 5.0 multiply_reduce_fusion
  317.6 2.2 broadcast.182
  319.8 174.8 %while.39 = (s32[]{:T(128)}, f32[128,1024]{0,1:T(8,128)S(1)}, f32[4,2048,128]{2,1,0:T(8,128)}, s32[]{:T(128)}, bf16[8,128,1024]{1,2,0:T(8,128)(2,1)}, /*index=5*...) while((s32[]{:T(128)}, f32[128,1024]{0,1:T(8,128)S(1)}, ...), condition=%wide.region_12.13_spmd.clone, body=%wide.region_9.12_spmd.clone.sunk | while | flops 1351823360 | bytes 85468640 | solution.py:221
  319.9 10.6 %conditional.7 = ((f32[128,1024]{0,1:T(8,128)S(1)}, f32[4,2048,128]{2,1,0:T(8,128)})) conditional(s32[]{:T(128)} %convert_element_type.142, (f32[128,1024]{0,1:T(8,128)S(1)}, f32[4,2048,128]{2,1,0:T(8,128)}) %tuple.111, (s32[]{:T(128)}, s32[]{:T(128)}, s32[2048]{0:T(1024)S(1)}, s32[128]{0:T(128)S(1)}, bf16[8,128,1024]{1,2,0:T(8,128)(2,1)}, ...), branch_computations={%region_10.10_spmd, %region_11.11_spmd.clone} | conditional | flops 1351428096 | bytes 81781416 | solution.py:217
  321.2 1.4 bitcast_select_fusion
  324.9 1.3 copy-done.3
  326.3 2.2 convolution_add_fusion
  328.5 1.9 copy-done.4
  330.5 14.3 %collective-permute-start.1 = (bf16[128,1024]{0,1:T(8,128)(2,1)S(1)}, bf16[128,1024]{0,1:T(8,128)(2,1)S(1)}, u32[]{:S(2)}, u32[]{:S(2)}) collective-permute-start(bf16[128,1024]{0,1:T(8,128)(2,1)S(1)} %convert_element_type.143), channel_id=1, source_target_pairs={{0,1},{1,2},{2,3},{3,4},{4,5},{5,6},{6,7},{7,0},{8,9},{9,10},{10,1... | collective-permute-start | bytes 786440 | tf_op jit(solution)/shard_map/while/body/eval_jaxpr/ppermute | solution.py:19
  344.8 42.4 %collective-permute-done.1 = bf16[128,1024]{0,1:T(8,128)(2,1)S(1)} collective-permute-done((bf16[128,1024]{0,1:T(8,128)(2,1)S(1)}, bf16[128,1024]{0,1:T(8,128)(2,1)S(1)}, u32[]{:S(2)}, u32[]{:S(2)}) %collective-permute-start.1) | collective-permute-done | bytes 262176 | tf_op jit(solution)/shard_map/while/body/eval_jaxpr/ppermute | solution.py:19
  387.4 13.8 %collective-permute-done.1 = bf16[128,1024]{0,1:T(8,128)(2,1)S(1)} collective-permute-done((bf16[128,1024]{0,1:T(8,128)(2,1)S(1)}, bf16[128,1024]{0,1:T(8,128)(2,1)S(1)}, u32[]{:S(2)}, u32[]{:S(2)}) %collective-permute-start.1) | collective-permute-done | bytes 262176 | tf_op jit(solution)/shard_map/while/body/eval_jaxpr/ppermute | solution.py:19
  401.5 13.8 %collective-permute-done.1 = bf16[128,1024]{0,1:T(8,128)(2,1)S(1)} collective-permute-done((bf16[128,1024]{0,1:T(8,128)(2,1)S(1)}, bf16[128,1024]{0,1:T(8,128)(2,1)S(1)}, u32[]{:S(2)}, u32[]{:S(2)}) %collective-permute-start.1) | collective-permute-done | bytes 262176 | tf_op jit(solution)/shard_map/while/body/eval_jaxpr/ppermute | solution.py:19
  415.6 13.8 %collective-permute-done.1 = bf16[128,1024]{0,1:T(8,128)(2,1)S(1)} collective-permute-done((bf16[128,1024]{0,1:T(8,128)(2,1)S(1)}, bf16[128,1024]{0,1:T(8,128)(2,1)S(1)}, u32[]{:S(2)}, u32[]{:S(2)}) %collective-permute-start.1) | collective-permute-done | bytes 262176 | tf_op jit(solution)/shard_map/while/body/eval_jaxpr/ppermute | solution.py:19
  429.7 14.8 %collective-permute-done.1 = bf16[128,1024]{0,1:T(8,128)(2,1)S(1)} collective-permute-done((bf16[128,1024]{0,1:T(8,128)(2,1)S(1)}, bf16[128,1024]{0,1:T(8,128)(2,1)S(1)}, u32[]{:S(2)}, u32[]{:S(2)}) %collective-permute-start.1) | collective-permute-done | bytes 262176 | tf_op jit(solution)/shard_map/while/body/eval_jaxpr/ppermute | solution.py:19
  444.9 16.3 %collective-permute-done.1 = bf16[128,1024]{0,1:T(8,128)(2,1)S(1)} collective-permute-done((bf16[128,1024]{0,1:T(8,128)(2,1)S(1)}, bf16[128,1024]{0,1:T(8,128)(2,1)S(1)}, u32[]{:S(2)}, u32[]{:S(2)}) %collective-permute-start.1) | collective-permute-done | bytes 262176 | tf_op jit(solution)/shard_map/while/body/eval_jaxpr/ppermute | solution.py:19
  461.4 16.3 %collective-permute-done.1 = bf16[128,1024]{0,1:T(8,128)(2,1)S(1)} collective-permute-done((bf16[128,1024]{0,1:T(8,128)(2,1)S(1)}, bf16[128,1024]{0,1:T(8,128)(2,1)S(1)}, u32[]{:S(2)}, u32[]{:S(2)}) %collective-permute-start.1) | collective-permute-done | bytes 262176 | tf_op jit(solution)/shard_map/while/body/eval_jaxpr/ppermute | solution.py:19
  478.0 16.3 %collective-permute-done.1 = bf16[128,1024]{0,1:T(8,128)(2,1)S(1)} collective-permute-done((bf16[128,1024]{0,1:T(8,128)(2,1)S(1)}, bf16[128,1024]{0,1:T(8,128)(2,1)S(1)}, u32[]{:S(2)}, u32[]{:S(2)}) %collective-permute-start.1) | collective-permute-done | bytes 262176 | tf_op jit(solution)/shard_map/while/body/eval_jaxpr/ppermute | solution.py:19
  495.8 5.6 convert_bitcast_fusion
  501.5 87.8 %reduce-scatter.5.cloned.1.call-done = bf16[512,1024]{0,1:T(8,128)(2,1)} async-done(((bf16[4096,1024]{0,1:T(8,128)(2,1)}), bf16[512,1024]{0,1:T(8,128)(2,1)}) %reduce-scatter.5.cloned.1.call-update) | async-done | bytes 1048592 | tf_op jit(solution)/shard_map/reduce_scatter | solution.py:237
  589.3 2.3 copy.128
  591.6 2.2 copy.135
  593.8 3.8 copy.105
  597.6 4.2 broadcast_in_dim_reshape.3
  601.7 2.8 multiply_convert_fusion
  604.5 1.4 copy.138
  605.9 2.3 convert_element_type.107
  608.2 9.0 %fusion.22 = bf16[1,128,4096]{2,1,0:T(8,128)(2,1)} fusion(bf16[2048,1024]{1,0:T(8,128)(2,1)} %collective-permute-done.6, bf16[2048,1024]{1,0:T(8,128)(2,1)} %maximum_select_fusion.1, pred[]{:T(512)S(6)} %eq.17, bf16[128,512]{0,1:T(8,128)(2,1)S(1)} %slice.61, bf16[128,512]{0,1:T(8,128)(2,1)S(1)} %bitcast.157), kind=kOutput, calls=%fused_computation.42 | convolution fusion | flops 1112539136 | bytes 9699329 | tf_op jit(solution)/shard_map/dot_general | solution.py:229
  617.2 1.4 reduce-scatter.7.cloned.1.call-done
  618.7 1.1 copy.129
  (156 shorter events, 20.6 us)
Async XLA Ops:
  7.2 582.2 %reduce-scatter.5.cloned.1.call-start = ((), (), s32[]{:S(2)}) async-start(), calls=%async_computation.2 | async-start | bytes 9437184 | tf_op jit(solution)/shard_map/reduce_scatter | solution.py:237
  7.2 1.9 collective-permute-start.2
  10.4 15.2 %collective-permute-start.3 = (bf16[256,1024]{1,0:T(8,128)(2,1)S(1)}, bf16[256,1024]{1,0:T(8,128)(2,1)S(1)}, u32[]{:S(2)}, u32[]{:S(2)}) collective-permute-start(bf16[256,1024]{1,0:T(8,128)(2,1)S(1)} %maximum_select_fusion.8), channel_id=1, source_target_pairs={{0,2},{1,3},{2,0},{3,1},{4,6},{5,7},{6,4},{7,5},{8,10},{9,11},{10,... | collective-permute-start | bytes 1572872 | tf_op jit(solution)/shard_map/ppermute | solution.py:70
  26.1 48.2 %collective-permute-start.4 = (bf16[512,1024]{1,0:T(8,128)(2,1)S(1)}, bf16[512,1024]{1,0:T(8,128)(2,1)}, u32[]{:S(2)}, u32[]{:S(2)}) collective-permute-start(bf16[512,1024]{1,0:T(8,128)(2,1)S(1)} %maximum_select_fusion.7), channel_id=1, source_target_pairs={{0,4},{1,5},{2,6},{3,7},{4,0},{5,1},{6,2},{7,3},{8,12},{9,13},{10,... | collective-permute-start | bytes 3145736 | tf_op jit(solution)/shard_map/ppermute | solution.py:70
  76.8 46.8 %collective-permute-start.5 = (bf16[1024,1024]{1,0:T(8,128)(2,1)S(1)}, bf16[1024,1024]{1,0:T(8,128)(2,1)}, u32[]{:S(2)}, u32[]{:S(2)}) collective-permute-start(bf16[1024,1024]{1,0:T(8,128)(2,1)S(1)} %maximum_select_fusion.2), channel_id=1, source_target_pairs={{0,8},{1,9},{2,10},{3,11},{4,12},{5,13},{6,14},{7,15},{8,0},{9,1},... | collective-permute-start | bytes 6291464 | tf_op jit(solution)/shard_map/ppermute | solution.py:70
  128.6 91.1 %collective-permute-start.6 = (bf16[2048,1024]{1,0:T(8,128)(2,1)}, bf16[2048,1024]{1,0:T(8,128)(2,1)}, u32[]{:S(2)}, u32[]{:S(2)}) collective-permute-start(bf16[2048,1024]{1,0:T(8,128)(2,1)} %maximum_select_fusion.1), channel_id=1, source_target_pairs={{0,16},{1,17},{2,18},{3,19},{4,20},{5,21},{6,22},{7,23},{8,24},{9,... | collective-permute-start | bytes 12582920 | tf_op jit(solution)/shard_map/ppermute | solution.py:70
  237.6 2.4 collective-permute-start
  240.0 17.8 %collective-permute-start = (bf16[128,1024]{0,1:T(8,128)(2,1)S(1)}, bf16[128,1024]{0,1:T(8,128)(2,1)S(1)}, u32[]{:S(2)}, u32[]{:S(2)}) collective-permute-start(bf16[128,1024]{0,1:T(8,128)(2,1)S(1)} %get-tuple-element.848), channel_id=1, source_target_pairs={{0,1},{1,2},{2,3},{3,4},{4,5},{5,6},{6,7},{8,9},{9,10},{10,11},{11... | collective-permute-start | bytes 786440 | tf_op jit(solution)/shard_map/while/body/eval_jaxpr/ppermute | solution.py:13
  257.9 7.7 %collective-permute-start = (bf16[128,1024]{0,1:T(8,128)(2,1)S(1)}, bf16[128,1024]{0,1:T(8,128)(2,1)S(1)}, u32[]{:S(2)}, u32[]{:S(2)}) collective-permute-start(bf16[128,1024]{0,1:T(8,128)(2,1)S(1)} %get-tuple-element.848), channel_id=1, source_target_pairs={{0,1},{1,2},{2,3},{3,4},{4,5},{5,6},{6,7},{8,9},{9,10},{10,11},{11... | collective-permute-start | bytes 786440 | tf_op jit(solution)/shard_map/while/body/eval_jaxpr/ppermute | solution.py:13
  265.6 17.3 %collective-permute-start = (bf16[128,1024]{0,1:T(8,128)(2,1)S(1)}, bf16[128,1024]{0,1:T(8,128)(2,1)S(1)}, u32[]{:S(2)}, u32[]{:S(2)}) collective-permute-start(bf16[128,1024]{0,1:T(8,128)(2,1)S(1)} %get-tuple-element.848), channel_id=1, source_target_pairs={{0,1},{1,2},{2,3},{3,4},{4,5},{5,6},{6,7},{8,9},{9,10},{10,11},{11... | collective-permute-start | bytes 786440 | tf_op jit(solution)/shard_map/while/body/eval_jaxpr/ppermute | solution.py:13
  283.0 7.7 %collective-permute-start = (bf16[128,1024]{0,1:T(8,128)(2,1)S(1)}, bf16[128,1024]{0,1:T(8,128)(2,1)S(1)}, u32[]{:S(2)}, u32[]{:S(2)}) collective-permute-start(bf16[128,1024]{0,1:T(8,128)(2,1)S(1)} %get-tuple-element.848), channel_id=1, source_target_pairs={{0,1},{1,2},{2,3},{3,4},{4,5},{5,6},{6,7},{8,9},{9,10},{10,11},{11... | collective-permute-start | bytes 786440 | tf_op jit(solution)/shard_map/while/body/eval_jaxpr/ppermute | solution.py:13
  290.7 8.5 %collective-permute-start = (bf16[128,1024]{0,1:T(8,128)(2,1)S(1)}, bf16[128,1024]{0,1:T(8,128)(2,1)S(1)}, u32[]{:S(2)}, u32[]{:S(2)}) collective-permute-start(bf16[128,1024]{0,1:T(8,128)(2,1)S(1)} %get-tuple-element.848), channel_id=1, source_target_pairs={{0,1},{1,2},{2,3},{3,4},{4,5},{5,6},{6,7},{8,9},{9,10},{10,11},{11... | collective-permute-start | bytes 786440 | tf_op jit(solution)/shard_map/while/body/eval_jaxpr/ppermute | solution.py:13
  299.3 7.7 %collective-permute-start = (bf16[128,1024]{0,1:T(8,128)(2,1)S(1)}, bf16[128,1024]{0,1:T(8,128)(2,1)S(1)}, u32[]{:S(2)}, u32[]{:S(2)}) collective-permute-start(bf16[128,1024]{0,1:T(8,128)(2,1)S(1)} %get-tuple-element.848), channel_id=1, source_target_pairs={{0,1},{1,2},{2,3},{3,4},{4,5},{5,6},{6,7},{8,9},{9,10},{10,11},{11... | collective-permute-start | bytes 786440 | tf_op jit(solution)/shard_map/while/body/eval_jaxpr/ppermute | solution.py:13
  319.8 175.2 %copy-start.6 = (f32[128,64]{1,0:T(8,128)S(1)}, f32[128,64]{1,0:T(8,128)}, u32[]{:S(2)}) copy-start(f32[128,64]{1,0:T(8,128)} %get-tuple-element.705) | copy-start | bytes 98308
  319.8 175.2 %copy-start.7 = (f32[128,64]{1,0:T(8,128)S(1)}, f32[128,64]{1,0:T(8,128)}, u32[]{:S(2)}) copy-start(f32[128,64]{1,0:T(8,128)} %get-tuple-element.706) | copy-start | bytes 98308
  320.9 1.7 copy-start
  324.1 2.2 copy-start.3
  328.5 1.9 copy-start.4
  330.5 56.7 %collective-permute-start.1 = (bf16[128,1024]{0,1:T(8,128)(2,1)S(1)}, bf16[128,1024]{0,1:T(8,128)(2,1)S(1)}, u32[]{:S(2)}, u32[]{:S(2)}) collective-permute-start(bf16[128,1024]{0,1:T(8,128)(2,1)S(1)} %convert_element_type.143), channel_id=1, source_target_pairs={{0,1},{1,2},{2,3},{3,4},{4,5},{5,6},{6,7},{7,0},{8,9},{9,10},{10,1... | collective-permute-start | bytes 786440 | tf_op jit(solution)/shard_map/while/body/eval_jaxpr/ppermute | solution.py:19
  387.3 13.9 %collective-permute-start.1 = (bf16[128,1024]{0,1:T(8,128)(2,1)S(1)}, bf16[128,1024]{0,1:T(8,128)(2,1)S(1)}, u32[]{:S(2)}, u32[]{:S(2)}) collective-permute-start(bf16[128,1024]{0,1:T(8,128)(2,1)S(1)} %convert_element_type.143), channel_id=1, source_target_pairs={{0,1},{1,2},{2,3},{3,4},{4,5},{5,6},{6,7},{7,0},{8,9},{9,10},{10,1... | collective-permute-start | bytes 786440 | tf_op jit(solution)/shard_map/while/body/eval_jaxpr/ppermute | solution.py:19
  401.5 13.9 %collective-permute-start.1 = (bf16[128,1024]{0,1:T(8,128)(2,1)S(1)}, bf16[128,1024]{0,1:T(8,128)(2,1)S(1)}, u32[]{:S(2)}, u32[]{:S(2)}) collective-permute-start(bf16[128,1024]{0,1:T(8,128)(2,1)S(1)} %convert_element_type.143), channel_id=1, source_target_pairs={{0,1},{1,2},{2,3},{3,4},{4,5},{5,6},{6,7},{7,0},{8,9},{9,10},{10,1... | collective-permute-start | bytes 786440 | tf_op jit(solution)/shard_map/while/body/eval_jaxpr/ppermute | solution.py:19
  415.6 13.9 %collective-permute-start.1 = (bf16[128,1024]{0,1:T(8,128)(2,1)S(1)}, bf16[128,1024]{0,1:T(8,128)(2,1)S(1)}, u32[]{:S(2)}, u32[]{:S(2)}) collective-permute-start(bf16[128,1024]{0,1:T(8,128)(2,1)S(1)} %convert_element_type.143), channel_id=1, source_target_pairs={{0,1},{1,2},{2,3},{3,4},{4,5},{5,6},{6,7},{7,0},{8,9},{9,10},{10,1... | collective-permute-start | bytes 786440 | tf_op jit(solution)/shard_map/while/body/eval_jaxpr/ppermute | solution.py:19
  429.7 14.9 %collective-permute-start.1 = (bf16[128,1024]{0,1:T(8,128)(2,1)S(1)}, bf16[128,1024]{0,1:T(8,128)(2,1)S(1)}, u32[]{:S(2)}, u32[]{:S(2)}) collective-permute-start(bf16[128,1024]{0,1:T(8,128)(2,1)S(1)} %convert_element_type.143), channel_id=1, source_target_pairs={{0,1},{1,2},{2,3},{3,4},{4,5},{5,6},{6,7},{7,0},{8,9},{9,10},{10,1... | collective-permute-start | bytes 786440 | tf_op jit(solution)/shard_map/while/body/eval_jaxpr/ppermute | solution.py:19
  444.8 16.4 %collective-permute-start.1 = (bf16[128,1024]{0,1:T(8,128)(2,1)S(1)}, bf16[128,1024]{0,1:T(8,128)(2,1)S(1)}, u32[]{:S(2)}, u32[]{:S(2)}) collective-permute-start(bf16[128,1024]{0,1:T(8,128)(2,1)S(1)} %convert_element_type.143), channel_id=1, source_target_pairs={{0,1},{1,2},{2,3},{3,4},{4,5},{5,6},{6,7},{7,0},{8,9},{9,10},{10,1... | collective-permute-start | bytes 786440 | tf_op jit(solution)/shard_map/while/body/eval_jaxpr/ppermute | solution.py:19
  461.4 16.4 %collective-permute-start.1 = (bf16[128,1024]{0,1:T(8,128)(2,1)S(1)}, bf16[128,1024]{0,1:T(8,128)(2,1)S(1)}, u32[]{:S(2)}, u32[]{:S(2)}) collective-permute-start(bf16[128,1024]{0,1:T(8,128)(2,1)S(1)} %convert_element_type.143), channel_id=1, source_target_pairs={{0,1},{1,2},{2,3},{3,4},{4,5},{5,6},{6,7},{7,0},{8,9},{9,10},{10,1... | collective-permute-start | bytes 786440 | tf_op jit(solution)/shard_map/while/body/eval_jaxpr/ppermute | solution.py:19
  478.0 16.4 %collective-permute-start.1 = (bf16[128,1024]{0,1:T(8,128)(2,1)S(1)}, bf16[128,1024]{0,1:T(8,128)(2,1)S(1)}, u32[]{:S(2)}, u32[]{:S(2)}) collective-permute-start(bf16[128,1024]{0,1:T(8,128)(2,1)S(1)} %convert_element_type.143), channel_id=1, source_target_pairs={{0,1},{1,2},{2,3},{3,4},{4,5},{5,6},{6,7},{7,0},{8,9},{9,10},{10,1... | collective-permute-start | bytes 786440 | tf_op jit(solution)/shard_map/while/body/eval_jaxpr/ppermute | solution.py:19
  494.6 1.2 copy-start.5
  501.4 117.2 %reduce-scatter.7.cloned.1.call-start = ((), (), s32[]{:S(2)}) async-start(), calls=%async_computation.3 | async-start | bytes 1310720
Sparse Core Ops, SparseCore 0:
  501.6 87.7 reduce-scatter.4
  592.2 26.4 reduce-scatter.6
